TPU v7x, 128 devices: a whole 4x4x4 slice. The times are simulated.
128 devices in a mesh: ctx: 8 (over y_hi, x), exp: 16 (over y_lo, z, core).
Axes of the slice: x: 4, y: 4 (y_hi: 2, y_lo: 2; y = y_hi * 2 + y_lo), z: 4, core: 2. Of those that a mesh axis runs over, the one named last changes fastest.
Arguments:
- queries: bfloat16 [16, 1024, 2048], P('exp', 'ctx'), may hold values from -6 to 6
- key_rows: bfloat16 [16, 1024, 256], P('exp', 'ctx'), may hold values from -6 to 6
- value_matrix: bfloat16 [16, 1024, 256], P('exp', 'ctx'), may hold values from -4 to 4
- hidden: bfloat16 [16, 1024, 2880], P('exp', 'ctx'), may hold values from -30 to 30
- out_weight: bfloat16 [2048, 2880], P('ctx'), may hold values from -0.125 to 0.125
- norm_gain: float32 [2880], replicated, may hold values from 0.1 to 1.9
- block_order: int32 [16], replicated, may hold values from 0 to 15, each once
- expert_ids: int32 [16, 1024, 4], P('exp', 'ctx'), may hold values from 0 to 63, all different within a row; in each aligned block of 128 rows (0 to 127, 128 to 255, ..., all dimensions but the last counted through in order) at most 16 rows name the same one
- route_weights: float32 [16, 1024, 4], P('exp', 'ctx'), may hold values from 0.1 to 0.6
- gate_up_weight: bfloat16 [128, 2880, 1440], P(('ctx', 'exp')), may hold values from -0.109375 to 0.109375
- down_weight: bfloat16 [128, 720, 2880], P(('ctx', 'exp')), may hold values from -0.15625 to 0.15625
Outputs:
- layer_out: bfloat16 [16, 1024, 2880], P('exp', 'ctx')
Inputs may be any that keep to these rules, and one draw needn't show every extreme that they name: `expert_ids`: the 128 rows of one device (aligned blocks of rows) name any one expert at most 16 times, a bound that some block reaches.
All inputs are finite; a program needn't handle non-finite values.
Results may differ from a plain program's by a relative error of at most 0.017.
Values may be sent and summed in bfloat16 or wider, within the bound.
A program may use at most 128 MiB of HBM per device.

v0:
```python
import jax
import jax.numpy as jnp
from jax import lax
from jax.sharding import PartitionSpec as P

D = 2880
QUERY_HEADS = 32
KEY_VALUE_HEADS = 4
HEAD_SIZE = 64
TOPK = 4
negative_large = -1e30


def expert_half(routed, gate_up, down_part):
    half_size = gate_up.shape[1] // 2
    gate_up_out = jnp.dot(routed, gate_up, preferred_element_type=jnp.float32)
    gate_part = gate_up_out[:, :half_size]
    up_part = gate_up_out[:, half_size:]
    activated = (gate_part * jax.nn.sigmoid(1.702 * gate_part) * (up_part + 1.0)).astype(
        jnp.bfloat16
    )
    return jnp.dot(activated, down_part, preferred_element_type=jnp.float32).astype(jnp.bfloat16)


def local(
    queries,
    key_rows,
    value_matrix,
    hidden,
    out_weight,
    norm_gain,
    block_order,
    expert_ids,
    route_weights,
    gate_up_weight,
    down_weight,
):
    ctx_count = lax.axis_size("ctx")
    exp_count = lax.axis_size("exp")
    token_count = queries.shape[1]
    block_len = token_count // 2
    query_group_size = QUERY_HEADS // KEY_VALUE_HEADS
    slot_ids = jnp.arange(2 * ctx_count, dtype=jnp.int32)

    def locate(row_index):
        table = (row_index // block_len)[:, None] == slot_ids[None, :]
        return (
            jnp.sum(jnp.where(table, block_order[None, :], 0), axis=1) * block_len
            + row_index % block_len
        )

    query_pos = locate(
        lax.axis_index("ctx") * token_count + jnp.arange(token_count, dtype=jnp.int32)
    )
    query_head_rows = queries[0].reshape(token_count, KEY_VALUE_HEADS, query_group_size, HEAD_SIZE)
    key_section = lax.all_gather(key_rows, "ctx", axis=1, tiled=True)
    value_section = lax.all_gather(value_matrix, "ctx", axis=1, tiled=True)
    section_length = key_section.shape[1]
    key_pos = locate(jnp.arange(section_length, dtype=jnp.int32))
    row_maximum = jnp.full(
        (KEY_VALUE_HEADS, query_group_size, token_count), negative_large, jnp.float32
    )
    key_head_rows = key_section[0].reshape(section_length, KEY_VALUE_HEADS, HEAD_SIZE)
    value_head_rows = value_section[0].reshape(section_length, KEY_VALUE_HEADS, HEAD_SIZE)
    scores = jnp.einsum(
        "qhgd,khd->hgqk", query_head_rows, key_head_rows, preferred_element_type=jnp.float32
    ) * HEAD_SIZE ** (-0.5)
    visible = key_pos[None, :] <= query_pos[:, None]
    masked = jnp.where(visible, scores, negative_large)
    new_max = jnp.maximum(row_maximum, jnp.max(masked, axis=-1))
    kept_probs = jnp.where(visible, jnp.exp(masked - new_max[..., None]), 0.0)
    row_total = jnp.sum(kept_probs, axis=-1)
    added = jnp.einsum(
        "hgqk,khd->qhgd",
        kept_probs.astype(jnp.bfloat16),
        value_head_rows,
        preferred_element_type=jnp.float32,
    )
    weighted_sum = added
    row_maximum, row_total, weighted_sum = (new_max, row_total, weighted_sum)
    attended = (
        (weighted_sum / jnp.transpose(row_total, (2, 0, 1))[..., None])
        .astype(jnp.bfloat16)
        .reshape(token_count, QUERY_HEADS * HEAD_SIZE)
    )
    projected = jnp.dot(
        attended,
        lax.all_gather(out_weight, "ctx", axis=0, tiled=True),
        preferred_element_type=jnp.float32,
    )
    residual = (hidden[0].astype(jnp.float32) + projected).astype(jnp.bfloat16)
    res_float = residual.astype(jnp.float32)
    moe_in = (
        res_float
        * lax.rsqrt(jnp.mean(res_float * res_float, axis=-1, keepdims=True) + 1e-05)
        * norm_gain
    ).astype(jnp.bfloat16)
    device_count = ctx_count * exp_count
    experts = device_count // 2
    capacity = 2 * token_count * TOPK // experts
    flat_ids = expert_ids[0].reshape(-1)
    onehot = (flat_ids[:, None] == jnp.arange(experts, dtype=jnp.int32)[None, :]).astype(jnp.int32)
    slot_index = jnp.sum((jnp.cumsum(onehot, axis=0) - 1) * onehot, axis=1)
    copies = jnp.repeat(moe_in, TOPK, axis=0)
    outgoing = jnp.zeros((experts, capacity, D), jnp.bfloat16).at[flat_ids, slot_index].set(copies)
    gate_up_local = gate_up_weight[0]
    down_local = down_weight[0]
    doubled = jnp.broadcast_to(outgoing[:, None], (experts, 2, capacity, D)).reshape(
        device_count, capacity, D
    )
    batch_rows = lax.all_to_all(doubled, ("ctx", "exp"), split_axis=0, concat_axis=0, tiled=True)
    flat_rows = batch_rows.reshape(-1, D)
    returned = lax.all_to_all(
        expert_half(flat_rows, gate_up_local, down_local).reshape(batch_rows.shape),
        ("ctx", "exp"),
        split_axis=0,
        concat_axis=0,
        tiled=True,
    )
    paired = returned.reshape(experts, 2, capacity, D)[flat_ids, :, slot_index]
    summed = (
        (paired[:, 0].astype(jnp.float32) + paired[:, 1].astype(jnp.float32))
        .astype(jnp.bfloat16)
        .astype(jnp.float32)
    )
    mixed = (
        (summed * route_weights[0].reshape(-1)[:, None]).reshape(token_count, TOPK, D).sum(axis=1)
    )
    return (res_float + mixed).astype(jnp.bfloat16)[None]


def solution(mesh):
    return jax.shard_map(
        local,
        mesh=mesh,
        in_specs=(
            P("exp", "ctx", None),
            P("exp", "ctx", None),
            P("exp", "ctx", None),
            P("exp", "ctx", None),
            P("ctx", None),
            P(),
            P(),
            P("exp", "ctx", None),
            P("exp", "ctx", None),
            P(("ctx", "exp"), None, None),
            P(("ctx", "exp"), None, None),
        ),
        out_specs=P("exp", "ctx", None),
        check_vma=False,
    )
```

profile of v0, /device:TPU:36, one launch (start us, length us, event | category | flops | bytes accessed | tf_op | source)
XLA Modules:
  0.0 783.1 jit_solution(11252463984967815645)
XLA Ops:
  8.4 34.9 %all_gather.9 = bf16[1,1024,256]{2,1,0:T(8,128)(2,1)S(1)} all-gather(bf16[1,128,256]{2,1,0:T(8,128)(2,1)} %param.12), channel_id=1, replica_groups=mesh['ctx'=8,'exp'=16] {'ctx'}, dimensions={1}, use_global_device_ids=true | all-gather | bytes 589824 | tf_op jit(solution)/shard_map/all_gather | solution.py:56
  44.9 36.4 %all_gather.10 = bf16[1,1024,256]{2,1,0:T(8,128)(2,1)S(1)} all-gather(bf16[1,128,256]{2,1,0:T(8,128)(2,1)} %param.13), channel_id=1, replica_groups=mesh['ctx'=8,'exp'=16] {'ctx'}, dimensions={1}, use_global_device_ids=true | all-gather | bytes 589824 | tf_op jit(solution)/shard_map/all_gather | solution.py:57
  84.1 2.4 fusion
  86.5 4.3 fusion.1
  90.8 4.0 divide_convert_fusion
  94.8 76.3 %all-gather.2.cloned.1.call-done = bf16[2048,2880]{0,1:T(8,128)(2,1)} async-done(((bf16[256,2880]{0,1:T(8,128)(2,1)}), bf16[2048,2880]{0,1:T(8,128)(2,1)}) %all-gather.2.cloned.1.call-update) | async-done | bytes 11796496 | tf_op jit(solution)/shard_map/all_gather | solution.py:88
  171.1 6.2 multiply_reduce_fusion.1
  179.3 2.4 broadcast_in_dim.80
  181.7 4.4 reshape.192
  186.1 3.0 broadcast_in_dim.79
  189.0 107.0 %scatter_fusion = bf16[64,16,2880]{2,1,0:T(8,128)(2,1)} fusion(bf16[64,16,2880]{2,1,0:T(8,128)(2,1)} %broadcast_in_dim.79, s32[512]{0:T(512)S(1)} %bitcast.74, bf16[512,2880]{1,0:T(8,128)(2,1)S(1)} %reshape.192), kind=kCustom, calls=%fused_computation.1 | custom fusion | bytes 8851456 | tf_op jit(solution)/shard_map/scatter | solution.py:105
  296.0 5.4 broadcast_in_dim.81
  301.4 146.1 %all_to_all.10 = bf16[128,16,2880]{2,1,0:T(8,128)(2,1)S(1)} all-to-all(bf16[128,16,2880]{2,1,0:T(8,128)(2,1)S(1)} %bitcast.73), channel_id=1, replica_groups=mesh['ctx'=8,'exp'=16] {'ctx','exp'}, dimensions={0} | all-to-all | bytes 23592960 | tf_op jit(solution)/shard_map/all_to_all | solution.py:111
  447.5 21.1 %fusion.3 = f32[2048,1440]{0,1:T(8,128)} fusion(bf16[2048,2880]{1,0:T(8,128)(2,1)S(1)} %bitcast.76, bf16[1,2880,1440]{1,2,0:T(8,128)(2,1)S(1)} %bitcast.84), kind=kOutput, calls=%fused_computation.8 | convolution fusion | flops 16986931200 | bytes 31887360 | tf_op jit(solution)/shard_map/dot_general | solution.py:16
  468.7 17.1 %convolution_convert_fusion = bf16[2048,2880]{0,1:T(8,128)(2,1)} fusion(bf16[1,720,2880]{2,1,0:T(8,128)(2,1)S(1)} %bitcast.86, f32[2048,1440]{0,1:T(8,128)} %fusion.3), kind=kOutput, calls=%fused_computation.7 | convolution fusion | flops 8511160320 | bytes 27740160 | tf_op jit(solution)/shard_map/dot_general | solution.py:22
  485.8 16.3 %copy.63 = bf16[2048,2880]{1,0:T(8,128)(2,1)} copy(bf16[2048,2880]{0,1:T(8,128)(2,1)} %convolution_convert_fusion) | data formatting | bytes 23592960 | tf_op jit(solution)/shard_map/convert_element_type | solution.py:22
  502.1 16.2 %all-to-all-start.1 = ((bf16[128,16,2880]{2,1,0:T(8,128)(2,1)}), bf16[128,16,2880]{2,1,0:T(8,128)(2,1)}, u32[]{:S(2)}, u32[]{:S(2)}) async-start(bf16[128,16,2880]{2,1,0:T(8,128)(2,1)} %bitcast.72), calls=%async_computation.1 | async-start | bytes 24117248 | tf_op jit(solution)/shard_map/all_to_all | solution.py:113
  518.5 172.9 %all-to-all-done.1 = bf16[128,16,2880]{2,1,0:T(8,128)(2,1)} async-done(((bf16[128,16,2880]{2,1,0:T(8,128)(2,1)}), bf16[128,16,2880]{2,1,0:T(8,128)(2,1)}, u32[]{:S(2)}, u32[]{:S(2)}) %all-to-all-start.1) | async-done | bytes 11796512 | tf_op jit(solution)/shard_map/all_to_all | solution.py:113
  691.4 18.0 %copy.64 = bf16[64,2,16,2880]{3,1,2,0:T(2,128)(2,1)} copy(bf16[64,2,16,2880]{3,2,1,0:T(8,128)(2,1)} %bitcast.20) | data formatting | bytes 23592960 | tf_op jit(solution)/shard_map/reshape | solution.py:120
  709.4 22.0 %gather_fusion = bf16[512,2,2880]{2,1,0:T(2,128)(2,1)} fusion(bf16[64,2,16,2880]{3,1,2,0:T(2,128)(2,1)} %copy.64, s32[512]{0:T(512)S(1)} %bitcast.75), kind=kCustom, calls=%fused_computation | custom fusion | bytes 11800576 | tf_op jit(solution)/shard_map/gather | solution.py:120
  731.4 26.1 %fusion.11 = f32[512,2880]{1,0:T(8,128)} fusion(bf16[512,2,2880]{2,1,0:T(2,128)(2,1)} %gather_fusion), kind=kLoop, calls=%fused_computation.16 | loop fusion | flops 7372800 | bytes 11796480 | tf_op jit(solution)/shard_map/convert_element_type | solution.py:124
  757.5 7.6 reshape.183
  765.2 7.1 multiply_reduce_fusion
  773.9 2.4 fusion.25
  (55 shorter events, 9.9 us)
Async XLA Ops:
  6.5 76.4 %copy-start.5 = (s32[16]{0:T(128)S(1)}, s32[16]{0:T(128)}, u32[]{:S(2)}) copy-start(s32[16]{0:T(128)} %param.17) | copy-start | bytes 196
  6.5 164.6 %all-gather.2.cloned.1.call-start = ((), (), s32[]{:S(2)}) async-start(), calls=%async_computation.2 | async-start | bytes 13271040 | tf_op jit(solution)/shard_map/all_gather | solution.py:88
  90.8 80.3 %copy-start.6 = (bf16[1,128,2880]{1,2,0:T(8,128)(2,1)S(1)}, bf16[1,128,2880]{1,2,0:T(8,128)(2,1)}, u32[]{:S(2)}) copy-start(bf16[1,128,2880]{1,2,0:T(8,128)(2,1)} %param.14) | copy-start | bytes 2211844
  171.1 7.4 copy-start.3
  177.3 1.2 copy-start.1
  296.0 151.5 %slice-start = ((s8[8478720]{0:T(1024)(128)(4,1)}), s8[4194304]{0:T(1024)(128)(4,1)S(1)}, s32[]{:S(2)}) async-start(s8[8478720]{0:T(1024)(128)(4,1)} %bitcast.83), calls=%async_computation.3 | async-start | bytes 8388608
  296.0 151.5 %slice-start.1 = ((s8[8478720]{0:T(1024)(128)(4,1)}), s8[4194304]{0:T(1024)(128)(4,1)S(1)}, s32[]{:S(2)}) async-start(s8[8478720]{0:T(1024)(128)(4,1)} %bitcast.83), calls=%async_computation.4 | async-start | bytes 8388608
  301.4 146.1 %slice-start.2 = ((s8[8478720]{0:T(1024)(128)(4,1)}), s8[90112]{0:T(1024)(128)(4,1)S(1)}, s32[]{:S(2)}) async-start(s8[8478720]{0:T(1024)(128)(4,1)} %bitcast.83), calls=%async_computation.5 | async-start | bytes 180224
  301.4 167.2 %slice-start.3 = ((s8[4239360]{0:T(1024)(128)(4,1)}), s8[4194304]{0:T(1024)(128)(4,1)S(1)}, s32[]{:S(2)}) async-start(s8[4239360]{0:T(1024)(128)(4,1)} %bitcast.85), calls=%async_computation.6 | async-start | bytes 8388608
  447.5 21.2 %slice-start.4 = ((s8[4239360]{0:T(1024)(128)(4,1)}), s8[45056]{0:T(1024)(128)(4,1)S(1)}, s32[]{:S(2)}) async-start(s8[4239360]{0:T(1024)(128)(4,1)} %bitcast.85), calls=%async_computation.7 | async-start | bytes 90112
  502.1 16.2 %copy-start.4 = (f32[1,128,4]{1,2,0:T(4,128)S(1)}, f32[1,128,4]{1,2,0:T(4,128)}, u32[]{:S(2)}) copy-start(f32[1,128,4]{1,2,0:T(4,128)} %param.19) | copy-start | bytes 6148
  502.1 189.3 %all-to-all-start.1 = ((bf16[128,16,2880]{2,1,0:T(8,128)(2,1)}), bf16[128,16,2880]{2,1,0:T(8,128)(2,1)}, u32[]{:S(2)}, u32[]{:S(2)}) async-start(bf16[128,16,2880]{2,1,0:T(8,128)(2,1)} %bitcast.72), calls=%async_computation.1 | async-start | bytes 24117248 | tf_op jit(solution)/shard_map/all_to_all | solution.py:113
  691.4 18.0 %copy-start = (s32[512,1]{0,1:T(1,128)S(1)}, s32[512,1]{0,1:T(1,128)}, u32[]{:S(2)}) copy-start(s32[512,1]{0,1:T(1,128)} %get-tuple-element.6) | copy-start | bytes 6148
  765.2 8.7 %copy-start.2 = (f32[128,2880]{0,1:T(8,128)S(1)}, f32[128,2880]{0,1:T(8,128)}, u32[]{:S(2)}) copy-start(f32[128,2880]{0,1:T(8,128)} %copy-done.1) | copy-start | bytes 4423684
Sparse Core Ops, SparseCore 0:
  9.5 161.5 all-gather.1
where the time goes:
time: 787 us; the launch traced here: 783 us
  waiting for transfers between devices  250 us (32%)
  blocking collectives  217 us (28%)
  local copies, waits for them, and re-layouts  192 us (24%)
  matrix products  50.8 us (6%)
  other arithmetic  42.7 us (5%)
  starting transfers between devices  16.2 us (2%)
  between operations  13.6 us (2%)
    all_to_all x1, waiting for transfers between devices, local(): lax.all_to_all(expert_half(flat_rows, gate_up_local, down_local).reshape(...  173 us
    all_to_all x1, blocking collectives, local(): lax.all_to_all(doubled, ('ctx', 'exp'), split_axis=0, concat_axis=0, tile...  146 us
    scatter x1, local copies, waits for them, and re-layouts, local(): jnp.zeros((experts, capacity, D), jnp.bfloat16).at[flat_ids, slot_index]  107 us
    all_gather x1, waiting for transfers between devices, local(): lax.all_gather(out_weight, 'ctx', axis=0, tiled=True)  76.3 us
    all_gather x1, blocking collectives, local(): value_section = lax.all_gather(value_matrix, 'ctx', axis=1, tiled=True)  36.4 us
    all_gather x1, blocking collectives, local(): key_section = lax.all_gather(key_rows, 'ctx', axis=1, tiled=True)  34.9 us
    convert_element_type x1, other arithmetic, local(): summed = (paired[:, 0].astype(jnp.float32) + paired[:, 1].astype(jnp.floa...  26.1 us
    gather x1, local copies, waits for them, and re-layouts, local(): paired = returned.reshape(experts, 2, capacity, D)[flat_ids, :, slot_index]  22 us
  transfers between devices with their start and end apart: 2, of which 2 were waited for; matrix products, arithmetic and copies ran while one was open for 2% of the time, Pallas kernels for 0%

commit v1 on v0

--- a/solution.py
+++ b/solution.py
@@ -53,8 +53,13 @@
         lax.axis_index("ctx") * token_count + jnp.arange(token_count, dtype=jnp.int32)
     )
     query_head_rows = queries[0].reshape(token_count, KEY_VALUE_HEADS, query_group_size, HEAD_SIZE)
-    key_section = lax.all_gather(key_rows, "ctx", axis=1, tiled=True)
-    value_section = lax.all_gather(value_matrix, "ctx", axis=1, tiled=True)
+    key_section, value_section = jnp.split(
+        lax.all_gather(
+            jnp.concatenate([key_rows, value_matrix], axis=0), "ctx", axis=1, tiled=True
+        ),
+        [key_rows.shape[0]],
+        axis=0,
+    )
     section_length = key_section.shape[1]
     key_pos = locate(jnp.arange(section_length, dtype=jnp.int32))
     row_maximum = jnp.full(

time: 787 us -> 829 us (1.053)
  waiting for transfers between devices: 250 us -> 360 us
  blocking collectives: 217 us -> 145 us
    all_gather x2 -> x0, blocking collectives: 71.3 us -> none  [the longest x1 36.4 us: local(): value_section = lax.all_gather(value_matrix, 'ctx', axis=1, tiled=True)]
    all_gather x1, waiting for transfers between devices: 76.3 us -> 144 us  [local(): lax.all_gather(out_weight, 'ctx', axis=0, tiled=True)]
    all_gather x0 -> x1, waiting for transfers between devices: none -> 42.1 us  [local(): lax.all_gather(jnp.concatenate([key_rows, value_matrix], axis=0), 'ctx',...]
  transfers between devices with their start and end apart: 2 -> 3, of which waited for: 2 -> 3; matrix products, arithmetic and copies ran while one was open for 2% -> 2% of each run, Pallas kernels for 0% -> 0%
where the time goes in v1:
time: 829 us; the launch traced here: 825 us
  waiting for transfers between devices  360 us (43%)
  local copies, waits for them, and re-layouts  194 us (23%)
  blocking collectives  145 us (17%)
  matrix products  50.8 us (6%)
  other arithmetic  45.7 us (6%)
  starting transfers between devices  16.3 us (2%)
  between operations  13.6 us (2%)
    all_to_all x1, waiting for transfers between devices, local(): lax.all_to_all(expert_half(flat_rows, gate_up_local, down_local).reshape(...  173 us
    all_to_all x1, blocking collectives, local(): lax.all_to_all(doubled, ('ctx', 'exp'), split_axis=0, concat_axis=0, tile...  145 us
    all_gather x1, waiting for transfers between devices, local(): lax.all_gather(out_weight, 'ctx', axis=0, tiled=True)  144 us
    scatter x1, local copies, waits for them, and re-layouts, local(): jnp.zeros((experts, capacity, D), jnp.bfloat16).at[flat_ids, slot_index]  107 us
    all_gather x1, waiting for transfers between devices, local(): lax.all_gather(jnp.concatenate([key_rows, value_matrix], axis=0), 'ctx',...  42.1 us
    convert_element_type x1, other arithmetic, local(): summed = (paired[:, 0].astype(jnp.float32) + paired[:, 1].astype(jnp.floa...  26.2 us
    gather x1, local copies, waits for them, and re-layouts, local(): paired = returned.reshape(experts, 2, capacity, D)[flat_ids, :, slot_index]  22 us
    dot_general x1, matrix products, expert_half(): gate_up_out = jnp.dot(routed, gate_up, preferred_element_type=jnp.float32)  21.2 us
  transfers between devices with their start and end apart: 3, of which 3 were waited for; matrix products, arithmetic and copies ran while one was open for 2% of the time, Pallas kernels for 0%

profile of v1, /device:TPU:36, one launch (start us, length us, event | category | flops | bytes accessed | tf_op | source)
XLA Modules:
  0.0 825.3 jit_solution(5507942562224787054)
XLA Ops:
  15.3 42.1 %all-gather.3.cloned.1.call-done = bf16[2,1024,256]{2,1,0:T(8,128)(2,1)} async-done(((bf16[2,128,256]{2,1,0:T(8,128)(2,1)}), bf16[2,1024,256]{2,1,0:T(8,128)(2,1)}) %all-gather.3.cloned.1.call-update) | async-done | bytes 1048592 | tf_op jit(solution)/shard_map/all_gather | solution.py:57
  59.1 2.4 fusion
  61.6 4.3 fusion.1
  65.9 4.0 divide_convert_fusion
  69.9 144.0 %all-gather.5.cloned.1.call-done = bf16[2048,2880]{0,1:T(8,128)(2,1)} async-done(((bf16[256,2880]{0,1:T(8,128)(2,1)}), bf16[2048,2880]{0,1:T(8,128)(2,1)}) %all-gather.5.cloned.1.call-update) | async-done | bytes 11796496 | tf_op jit(solution)/shard_map/all_gather | solution.py:93
  213.8 6.2 multiply_reduce_fusion.1
  222.0 2.4 broadcast_in_dim.80
  224.4 4.4 reshape.192
  228.8 3.0 broadcast_in_dim.79
  231.8 107.0 %scatter_fusion = bf16[64,16,2880]{2,1,0:T(8,128)(2,1)} fusion(bf16[64,16,2880]{2,1,0:T(8,128)(2,1)} %broadcast_in_dim.79, s32[512]{0:T(512)S(1)} %bitcast.74, bf16[512,2880]{1,0:T(8,128)(2,1)S(1)} %reshape.192), kind=kCustom, calls=%fused_computation.1 | custom fusion | bytes 8851456 | tf_op jit(solution)/shard_map/scatter | solution.py:110
  338.7 5.4 broadcast_in_dim.81
  344.2 145.4 %all_to_all.10 = bf16[128,16,2880]{2,1,0:T(8,128)(2,1)S(1)} all-to-all(bf16[128,16,2880]{2,1,0:T(8,128)(2,1)S(1)} %bitcast.73), channel_id=1, replica_groups=mesh['ctx'=8,'exp'=16] {'ctx','exp'}, dimensions={0} | all-to-all | bytes 23592960 | tf_op jit(solution)/shard_map/all_to_all | solution.py:116
  489.6 21.2 %fusion.3 = f32[2048,1440]{0,1:T(8,128)} fusion(bf16[2048,2880]{1,0:T(8,128)(2,1)S(1)} %bitcast.76, bf16[1,2880,1440]{1,2,0:T(8,128)(2,1)S(1)} %bitcast.84), kind=kOutput, calls=%fused_computation.8 | convolution fusion | flops 16986931200 | bytes 31887360 | tf_op jit(solution)/shard_map/dot_general | solution.py:16
  510.8 17.1 %convolution_convert_fusion = bf16[2048,2880]{0,1:T(8,128)(2,1)} fusion(bf16[1,720,2880]{2,1,0:T(8,128)(2,1)S(1)} %bitcast.86, f32[2048,1440]{0,1:T(8,128)} %fusion.3), kind=kOutput, calls=%fused_computation.7 | convolution fusion | flops 8511160320 | bytes 27740160 | tf_op jit(solution)/shard_map/dot_general | solution.py:22
  527.9 16.3 %copy.63 = bf16[2048,2880]{1,0:T(8,128)(2,1)} copy(bf16[2048,2880]{0,1:T(8,128)(2,1)} %convolution_convert_fusion) | data formatting | bytes 23592960 | tf_op jit(solution)/shard_map/convert_element_type | solution.py:22
  544.2 16.2 %all-to-all-start.1 = ((bf16[128,16,2880]{2,1,0:T(8,128)(2,1)}), bf16[128,16,2880]{2,1,0:T(8,128)(2,1)}, u32[]{:S(2)}, u32[]{:S(2)}) async-start(bf16[128,16,2880]{2,1,0:T(8,128)(2,1)} %bitcast.72), calls=%async_computation.1 | async-start | bytes 24117248 | tf_op jit(solution)/shard_map/all_to_all | solution.py:118
  560.6 172.9 %all-to-all-done.1 = bf16[128,16,2880]{2,1,0:T(8,128)(2,1)} async-done(((bf16[128,16,2880]{2,1,0:T(8,128)(2,1)}), bf16[128,16,2880]{2,1,0:T(8,128)(2,1)}, u32[]{:S(2)}, u32[]{:S(2)}) %all-to-all-start.1) | async-done | bytes 11796512 | tf_op jit(solution)/shard_map/all_to_all | solution.py:118
  733.5 18.0 %copy.64 = bf16[64,2,16,2880]{3,1,2,0:T(2,128)(2,1)} copy(bf16[64,2,16,2880]{3,2,1,0:T(8,128)(2,1)} %bitcast.20) | data formatting | bytes 23592960 | tf_op jit(solution)/shard_map/reshape | solution.py:125
  751.5 22.0 %gather_fusion = bf16[512,2,2880]{2,1,0:T(2,128)(2,1)} fusion(bf16[64,2,16,2880]{3,1,2,0:T(2,128)(2,1)} %copy.64, s32[512]{0:T(512)S(1)} %bitcast.75), kind=kCustom, calls=%fused_computation | custom fusion | bytes 11800576 | tf_op jit(solution)/shard_map/gather | solution.py:125
  773.6 26.2 %fusion.11 = f32[512,2880]{1,0:T(8,128)} fusion(bf16[512,2,2880]{2,1,0:T(2,128)(2,1)} %gather_fusion), kind=kLoop, calls=%fused_computation.16 | loop fusion | flops 7372800 | bytes 11796480 | tf_op jit(solution)/shard_map/convert_element_type | solution.py:129
  799.8 7.6 reshape.183
  807.4 7.1 multiply_reduce_fusion
  814.5 1.6 copy.66
  816.1 2.4 fusion.25
  (56 shorter events, 12.5 us)
Async XLA Ops:
  6.5 50.9 %all-gather.3.cloned.1.call-start = ((), (), s32[]{:S(2)}) async-start(), calls=%async_computation.2 | async-start | bytes 1179648 | tf_op jit(solution)/shard_map/all_gather | solution.py:57
  8.1 205.7 %all-gather.5.cloned.1.call-start = ((), (), s32[]{:S(2)}) async-start(), calls=%async_computation.3 | async-start | bytes 13271040 | tf_op jit(solution)/shard_map/all_gather | solution.py:93
  65.9 148.0 %copy-start.5 = (bf16[1,128,2880]{1,2,0:T(8,128)(2,1)S(1)}, bf16[1,128,2880]{1,2,0:T(8,128)(2,1)}, u32[]{:S(2)}) copy-start(bf16[1,128,2880]{1,2,0:T(8,128)(2,1)} %param.14) | copy-start | bytes 2211844
  213.8 7.4 copy-start.3
  220.0 1.2 copy-start.1
  338.7 150.8 %slice-start = ((s8[8478720]{0:T(1024)(128)(4,1)}), s8[4194304]{0:T(1024)(128)(4,1)S(1)}, s32[]{:S(2)}) async-start(s8[8478720]{0:T(1024)(128)(4,1)} %bitcast.83), calls=%async_computation.4 | async-start | bytes 8388608
  338.7 150.8 %slice-start.1 = ((s8[8478720]{0:T(1024)(128)(4,1)}), s8[4194304]{0:T(1024)(128)(4,1)S(1)}, s32[]{:S(2)}) async-start(s8[8478720]{0:T(1024)(128)(4,1)} %bitcast.83), calls=%async_computation.5 | async-start | bytes 8388608
  344.1 145.4 %slice-start.2 = ((s8[8478720]{0:T(1024)(128)(4,1)}), s8[90112]{0:T(1024)(128)(4,1)S(1)}, s32[]{:S(2)}) async-start(s8[8478720]{0:T(1024)(128)(4,1)} %bitcast.83), calls=%async_computation.6 | async-start | bytes 180224
  344.1 166.7 %slice-start.3 = ((s8[4239360]{0:T(1024)(128)(4,1)}), s8[4194304]{0:T(1024)(128)(4,1)S(1)}, s32[]{:S(2)}) async-start(s8[4239360]{0:T(1024)(128)(4,1)} %bitcast.85), calls=%async_computation.7 | async-start | bytes 8388608
  489.6 21.2 %slice-start.4 = ((s8[4239360]{0:T(1024)(128)(4,1)}), s8[45056]{0:T(1024)(128)(4,1)S(1)}, s32[]{:S(2)}) async-start(s8[4239360]{0:T(1024)(128)(4,1)} %bitcast.85), calls=%async_computation.8 | async-start | bytes 90112
  544.2 16.2 %copy-start.4 = (f32[1,128,4]{1,2,0:T(4,128)S(1)}, f32[1,128,4]{1,2,0:T(4,128)}, u32[]{:S(2)}) copy-start(f32[1,128,4]{1,2,0:T(4,128)} %param.19) | copy-start | bytes 6148
  544.2 189.3 %all-to-all-start.1 = ((bf16[128,16,2880]{2,1,0:T(8,128)(2,1)}), bf16[128,16,2880]{2,1,0:T(8,128)(2,1)}, u32[]{:S(2)}, u32[]{:S(2)}) async-start(bf16[128,16,2880]{2,1,0:T(8,128)(2,1)} %bitcast.72), calls=%async_computation.1 | async-start | bytes 24117248 | tf_op jit(solution)/shard_map/all_to_all | solution.py:118
  733.5 18.0 %copy-start = (s32[512,1]{0,1:T(1,128)S(1)}, s32[512,1]{0,1:T(1,128)}, u32[]{:S(2)}) copy-start(s32[512,1]{0,1:T(1,128)} %get-tuple-element.6) | copy-start | bytes 6148
  807.4 8.7 %copy-start.2 = (f32[128,2880]{0,1:T(8,128)S(1)}, f32[128,2880]{0,1:T(8,128)}, u32[]{:S(2)}) copy-start(f32[128,2880]{0,1:T(8,128)} %copy-done.1) | copy-start | bytes 4423684
Sparse Core Ops, SparseCore 0:
  9.7 47.6 all-gather.2
  59.6 154.1 all-gather.4
